TPU v7x, 512 devices: a whole 4x8x8 slice. The times are simulated.
512 devices in a mesh: pair: 2 (over core), box: 16 (over z_hi, x), tile: 16 (over z_lo, y).
Axes of the slice: x: 4, y: 8, z: 8 (z_hi: 4, z_lo: 2; z = z_hi * 2 + z_lo), core: 2. Of those that a mesh axis runs over, the one named last changes fastest.
Arguments:
- child_maps: bfloat16 [2, 256, 1152, 1152], P('pair', ('box', 'tile')), parts along dimension 1, as said below
- face_order: int32 [16, 2, 6], P('box'), parts along dimension 0, may hold values from 0 to 5, each once within a row
Outputs:
- parent_update: bfloat16 [2, 256, 960, 768], P('pair', ('box', 'tile')), parts along dimension 1
There are 16 independent parts, one for each index of `box`. A program takes and returns all parts, laid end to end along the dimension named above; each array names one. Nothing has to cross between parts.
Inputs may be any that keep to these rules, and one draw needn't show every extreme that they name: Each row of face_order lists every face once: entry 0 is the child's shared face, entries 1 to 5 its exterior faces in parent order. `child_maps`: child maps are dense with independent entries.
All inputs are finite; a program needn't handle non-finite values.
Results may differ from a plain program's by a relative error of at most 0.012.
Values may be sent and summed in bfloat16 or wider, within the bound.
No kernel may reach another device: no remote copies, remote signals or barrier semaphores. Data moves between devices by JAX's collectives and lax.ppermute only.
A program may use at most 64 MiB of HBM per device.

v0:
```python
import math

import jax
import jax.numpy as jnp
from jax import lax
from jax.experimental import pallas as pl
from jax.experimental.pallas import tpu as pltpu
from jax.sharding import PartitionSpec as P

FACE = 768
FACES = 6
CF = 2
PIECE = 192
LANES = 128
HALF = PIECE // 2
TILE_ROWS = PIECE + HALF
WIN_ROWS = CF * PIECE * PIECE // LANES
RING = 8
EXT = FACES - 1
EXT_ROWS = EXT * TILE_ROWS
EXT_SHAPE = (EXT_ROWS, LANES)


def ext_store(out, rows, value):
    out[rows, :] = value


def dot(a, b):
    return jnp.dot(a, b, preferred_element_type=jnp.float32)


def one_hot(condition):
    return jnp.where(condition, 1.0, 0.0).astype(jnp.bfloat16)


def packers(shift, odd_col):
    r = lax.broadcasted_iota(jnp.int32, (256, 256), 0)
    c = lax.broadcasted_iota(jnp.int32, (256, 256), 1)
    first = (c < LANES) & (r == c + shift)

    def rest(offset):
        q = c - LANES - offset
        return one_hot(first | ((q >= 0) & (q < 64) & (r == q + LANES + shift)))

    return rest(64 * odd_col), rest(64 * (1 - odd_col))


def pack(ca, cb, starts, shift, odd_col):
    q_top, q_bottom = packers(shift, odd_col)

    def half(offset):
        rows = [pl.ds(pl.multiple_of(start + offset, HALF), HALF) for start in starts]
        return jnp.concatenate([jnp.concatenate([ca[at, :], cb[at, :]], axis=1) for at in rows], axis=0)

    top, bottom = dot(half(0), q_top), dot(half(HALF), q_bottom)
    packed = []
    for m in range(len(starts)):
        rows = slice(m * HALF, (m + 1) * HALF)
        left = jnp.concatenate([top[rows, :LANES], bottom[rows, :LANES]], axis=0)
        packed.append((left.astype(jnp.bfloat16), (top[rows, LANES:] + bottom[rows, LANES:]).astype(jnp.bfloat16)))
    return packed


def here():
    return lax.axis_index("pair"), lax.axis_index("tile")


def shared_kernel(face, ca, cb, out):
    pair, tile = here()
    ((left, rest),) = pack(ca, cb, [0], 64 * (face[pair, 0] & 1), tile & 1)
    for n in range(RING):
        out[n, :PIECE] = left
        out[n, PIECE:] = rest


def edges_kernel(face, ca, cb, w0a, w0b, w1a, w1b, win_out, ext_out):
    pair, tile = here()
    starts = [face[pair, m + 1] * PIECE for m in range(EXT)]
    for m, (left, rest) in enumerate(pack(ca, cb, starts, 64 * (face[pair, 0] & 1), tile & 1)):
        ext_store(ext_out, slice(m * PIECE, (m + 1) * PIECE), left)
        ext_store(ext_out, slice(EXT * PIECE + m * HALF, EXT * PIECE + (m + 1) * HALF), rest)
    r = lax.broadcasted_iota(jnp.int32, (256, CF * PIECE), 0)
    c = lax.broadcasted_iota(jnp.int32, (256, CF * PIECE), 1)
    total = None
    for n, (a, b) in enumerate(((w0a, w0b), (w1a, w1b))):
        q = c - n * PIECE
        move = one_hot((q >= 0) & (q < PIECE) & (r == q + 64 * (face[pair, 1 + n] & 1)))
        part = dot(jnp.concatenate([a[...], b[...]], axis=1), move)
        total = part if total is None else total + part
    for n in range(3):
        win_out[n * PIECE : (n + 1) * PIECE, :] = total[:, n * LANES : (n + 1) * LANES].astype(jnp.bfloat16)


def column(rows, order, step, block):
    def index(g, face):
        faces = face.at[lax.axis_index("pair")]
        return faces[0] if block else 0, (faces[order] * PIECE) // LANES + step

    return pl.BlockSpec((rows, LANES), index)


def extraction(kernel, in_specs, shapes, cost):
    return pl.pallas_call(
        kernel,
        grid_spec=pltpu.PrefetchScalarGridSpec(
            num_scalar_prefetch=1,
            grid=(1,),
            in_specs=in_specs,
            out_specs=[pl.BlockSpec(shape, lambda g, f, d=len(shape): (0,) * d) for shape in shapes],
        ),
        out_shape=[jax.ShapeDtypeStruct(shape, jnp.bfloat16) for shape in shapes],
        cost_estimate=cost,
    )


def extract_shared(tile, face):
    specs = [column(PIECE, 0, step, True) for step in range(2)]
    cost = pl.CostEstimate(flops=3 * 10**7, bytes_accessed=10**6, transcendentals=0)
    return extraction(shared_kernel, specs, [(RING, TILE_ROWS, LANES)], cost)(face, tile, tile)[0]


def extract_edges(tile, face):
    specs = [column(tile.shape[0], 0, step, False) for step in range(2)]
    specs += [column(PIECE, 1 + n, step, True) for n in range(CF) for step in range(2)]
    shapes = [(WIN_ROWS, LANES), EXT_SHAPE]
    cost = pl.CostEstimate(flops=4 * 10**8, bytes_accessed=2 * 10**6, transcendentals=0)
    return extraction(edges_kernel, specs, shapes, cost)(face, *[tile] * 6)


def main_at(index, own_col):
    return pl.multiple_of(LANES * (index ^ own_col), LANES)


def rest_at(index, own_col):
    return pl.multiple_of(4 * LANES + LANES * ((index ^ own_col) >> 1) + 64 * (index & 1), 64)


def swap_halves(x):
    return jnp.concatenate([x[:, 64:], x[:, :64]], axis=1)


def place_tile(source, n, target, rests, row, col, own_col):
    lanes = pl.ds(main_at(col, own_col), LANES)
    target[pl.ds(main_at(row, own_col), LANES), lanes] = source[n, :LANES]
    target[pl.ds(rest_at(row, own_col), 64), lanes] = source[n, LANES:PIECE]
    rests[row, col] = source[n, PIECE:]


def join_rests(target, rests, own_col):
    left = lax.broadcasted_iota(jnp.int32, (HALF, LANES), 1) < 64

    def body(step, carry):
        row, two = step // 2, step % 2
        even, odd = rests[row, 2 * two], rests[row, 2 * two + 1]
        lanes = pl.ds(pl.multiple_of(4 * LANES + LANES * (two ^ (own_col >> 1)), LANES), LANES)
        top = jnp.where(left, even, odd)
        bottom = swap_halves(jnp.where(left, odd, even))
        start = main_at(row, own_col)
        target[pl.ds(start, HALF), lanes] = top
        target[pl.ds(pl.multiple_of(start + HALF, 32), LANES - HALF), lanes] = bottom[: LANES - HALF]
        target[pl.ds(rest_at(row, own_col), 64), lanes] = bottom[LANES - HALF :]
        return carry

    lax.fori_loop(0, 8, body, 0)


def series_kernel(own, far, p_own, p_far, win, w4, zv, zw, pxw, out, *scratch):
    mine, other, rests, power, power2, start_a, total = scratch
    pair, tile = here()
    z = tile >> 3
    own_col = tile & 3
    own_row = tile >> 2

    def place(target, near, far):
        for plane, parts in ((z, near), (1 - z, far)):
            for n in range(RING):
                place_tile(parts, n, target, rests, 2 * plane + n // 4, n % 4, own_col)
        join_rests(target, rests, own_col)

    def place_window(lane_half, sources, target):
        for n, (source, base) in enumerate(sources):
            row = own_row ^ n
            for piece in range(3):
                at = base + piece * PIECE
                lanes = lane_half(piece)
                target[pl.ds(main_at(row, own_col), LANES), lanes] = source[at : at + LANES, :]
                target[pl.ds(rest_at(row, own_col), 64), lanes] = source[at + LANES : at + PIECE, :]

    win_sources = (
        [(x, 0) for x in (win, w4, zv, zw)],
        [(pxw, n * WIN_ROWS) for n in range(4)],
    )
    place(mine, own, far)
    place(other, p_own, p_far)
    half = CF * PIECE
    my_half = pair * half
    place_window(lambda p: pl.ds(p * LANES, LANES), win_sources[0], start_a)
    place_window(lambda p: pl.ds(pl.multiple_of(half - my_half + p * LANES, LANES), LANES), win_sources[1], total)

    lanes = pl.ds(pl.multiple_of(my_half, LANES), half)
    power[...] = dot(other[...], mine[...]).astype(jnp.bfloat16)
    total[:, lanes] = dot(other[...], start_a[...]).astype(jnp.bfloat16)

    def add(matrix, source, target):
        target[...] = (source[...].astype(jnp.float32) + dot(matrix[...], source[...])).astype(jnp.bfloat16)

    power2[...] = dot(power[...], power[...]).astype(jnp.bfloat16)
    add(power, total, mine)
    add(power2, mine, other)
    power[...] = dot(power2[...], power2[...]).astype(jnp.bfloat16)
    add(power, other, out)


def series(lists):
    vmem = pl.BlockSpec(memory_space=pltpu.VMEM)
    square = pltpu.VMEM((FACE, FACE), jnp.bfloat16)
    return pl.pallas_call(
        series_kernel,
        in_specs=[vmem] * len(lists),
        out_specs=vmem,
        out_shape=jax.ShapeDtypeStruct((FACE, FACE), jnp.bfloat16),
        scratch_shapes=[
            square,
            square,
            pltpu.VMEM((4, 4, HALF, LANES), jnp.bfloat16),
            square,
            square,
            pltpu.VMEM((FACE, CF * PIECE), jnp.bfloat16),
            square,
        ],
        cost_estimate=pl.CostEstimate(flops=6 * 10**9, bytes_accessed=6 * 10**6, transcendentals=0),
        compiler_params=pltpu.CompilerParams(vmem_limit_bytes=40 * 2**20),
        name="series",
    )(*lists)


def update_kernel(e0, e1, e2, near, relayed, factor, out, matrix):
    col = here()[1] & 3
    inner = ((col ^ (col >> 1)) & 1) == 1
    left = (lax.broadcasted_iota(jnp.int32, (HALF, LANES), 1) < 64) ^ ((col & 1) == 1)
    main = EXT * PIECE

    def fill(two, a, b):
        for n, e in enumerate((a, b)):
            matrix[:, (2 * two + n) * LANES : (2 * two + n + 1) * LANES] = e[:main, :]
        lanes = slice((4 + two) * LANES, (5 + two) * LANES)
        for m in range(EXT):
            x = a[main + m * HALF : main + (m + 1) * HALF, :]
            v = b[main + m * HALF : main + (m + 1) * HALF, :]
            matrix[m * PIECE : m * PIECE + HALF, lanes] = jnp.where(left, x, v)
            matrix[m * PIECE + HALF : (m + 1) * PIECE, lanes] = swap_halves(jnp.where(left, v, x))

    fill(0, e0, e1)

    @pl.when(inner)
    def _():
        fill(1, e2, near)

    @pl.when(jnp.logical_not(inner))
    def _():
        fill(1, e2, relayed)

    for m in range(2):
        rows = slice(m * main // 2, (m + 1) * main // 2)
        out[rows, :] = (dot(matrix[rows, :], factor[...]) * math.sqrt(FACE)).astype(jnp.bfloat16)


def update(chunks, factor):
    vmem = pl.BlockSpec(memory_space=pltpu.VMEM)
    return pl.pallas_call(
        update_kernel,
        in_specs=[vmem] * (len(chunks) + 1),
        out_specs=vmem,
        out_shape=jax.ShapeDtypeStruct((EXT * PIECE, FACE), jnp.bfloat16),
        scratch_shapes=[pltpu.VMEM((EXT * PIECE, FACE), jnp.bfloat16)],
        cost_estimate=pl.CostEstimate(flops=1130 * 10**6, bytes_accessed=4 * 10**6, transcendentals=0),
        compiler_params=pltpu.CompilerParams(vmem_limit_bytes=32 * 2**20),
        name="update",
    )(*chunks, factor)


def permute(value, pairs, axis="tile"):
    return lax.ppermute(value, axis, pairs)


def masked(mask):
    return [(source, source ^ mask) for source in range(16)]


def ring_gather(copies):
    groups = [[RING * z + y for y in range(RING)] for z in range(2)]
    return lax.all_to_all(copies, "tile", 0, 0, axis_index_groups=groups, tiled=True)


def in_rows(steps):
    return [(4 * row + a, 4 * row + b) for row in range(4) for a, b in steps]


def program(child_maps, face_order):
    inner, outer = in_rows(((1, 2), (2, 1))), in_rows(((1, 0), (2, 3)))
    partner = [(0, 1), (1, 0)]
    own = ring_gather(extract_shared(child_maps[0, 0], face_order[0]))
    win, ext = extract_edges(child_maps[0, 0], face_order[0])
    w4 = permute(win, masked(4))
    e2 = permute(ext, masked(2))
    zv = permute(win, masked(8))
    zw = permute(w4, masked(8))
    e1 = permute(ext, masked(1))
    pxw = permute(jnp.concatenate([win, w4, zv, zw]), partner, "pair")
    far = permute(own, masked(8))
    p_own = permute(own, partner, "pair")
    p_far = permute(far, partner, "pair")
    near = permute(ext, inner)
    relayed = permute(e2, outer)
    factor = series([own, far, p_own, p_far, win, w4, zv, zw, pxw])
    return update([ext, e1, e2, near, relayed], factor)[None, None]


def solution(mesh):
    return jax.shard_map(
        program,
        mesh=mesh,
        in_specs=(P("pair", ("box", "tile"), None, None), P("box", None, None)),
        out_specs=P("pair", ("box", "tile"), None, None),
        check_vma=False,
    )
```

profile of v0, /device:TPU:1, one launch (start us, length us, event | category | flops | bytes accessed | tf_op | source)
XLA Modules:
  0.0 95.4 jit_solution(10887524161944628085)
XLA Ops:
  0.0 2.6 %shard_map.29 = bf16[8,288,128]{2,1,0:T(8,128)(2,1)} custom-call(s32[2,6]{1,0:T(2,128)} %bitcast.11, bf16[1152,1152]{1,0:T(8,128)(2,1)} %bitcast.3, bf16[1152,1152]{1,0:T(8,128)(2,1)} %bitcast.4), custom_call_target="tpu_custom_call" | custom-call | flops 30000000 | bytes 1000000 | tf_op jit(solution)/shard_map/pallas_call | solution.py:119
  2.6 7.6 %all-to-all-start = ((bf16[8,288,128]{2,1,0:T(8,128)(2,1)}), bf16[8,288,128]{2,1,0:T(8,128)(2,1)S(1)}, u32[]{:S(2)}, u32[]{:S(2)}) async-start(bf16[8,288,128]{2,1,0:T(8,128)(2,1)} %shard_map.29), calls=%async_computation | async-start | bytes 1179648 | tf_op jit(solution)/shard_map/all_to_all | solution.py:292
  10.2 2.9 %shard_map.28 = (bf16[576,128]{1,0:T(8,128)(2,1)}, bf16[1440,128]{1,0:T(8,128)(2,1)}) custom-call(s32[2,6]{1,0:T(2,128)} %bitcast.12, bf16[1152,1152]{1,0:T(8,128)(2,1)} %bitcast.5, bf16[1152,1152]{1,0:T(8,128)(2,1)} %bitcast.6, bf16[1152,1152]{1,0:T(8,128)(2,1)} %bitcast.7, bf16[1152,1152]{1,0:T(8,128)(2,1)} %bitcast.8, bf16[1152,1152]{1,0:T(8,128)(2,1)} %bitcast.9, ...), custom_call_target="tpu_custom_call" | custom-call | flops 400000000 | bytes 2000000 | tf_op jit(solution)/shard_map/pallas_call | solution.py:127
  13.2 0.0 copy-start
  13.2 0.0 copy-start.1
  13.2 7.4 %collective-permute-start.7 = (bf16[576,128]{1,0:T(8,128)(2,1)}, bf16[576,128]{1,0:T(8,128)(2,1)S(1)}, u32[]{:S(2)}, u32[]{:S(2)}) collective-permute-start(bf16[576,128]{1,0:T(8,128)(2,1)} %get-tuple-element.8.win), channel_id=1, source_target_pairs={{0,4},{1,5},{2,6},{3,7},{4,0},{5,1},{6,2},{7,3},{8,12},{9,13},{10,... | collective-permute-start | bytes 442376 | tf_op jit(solution)/shard_map/ppermute | solution.py:283
  20.6 6.3 %all-to-all-done.own = bf16[8,288,128]{2,1,0:T(8,128)(2,1)S(1)} async-done(((bf16[8,288,128]{2,1,0:T(8,128)(2,1)}), bf16[8,288,128]{2,1,0:T(8,128)(2,1)S(1)}, u32[]{:S(2)}, u32[]{:S(2)}) %all-to-all-start) | async-done | bytes 589856 | tf_op jit(solution)/shard_map/all_to_all | solution.py:292
  26.9 5.5 %collective-permute-start.4 = (bf16[8,288,128]{2,1,0:T(8,128)(2,1)S(1)}, bf16[8,288,128]{2,1,0:T(8,128)(2,1)S(1)}, u32[]{:S(2)}, u32[]{:S(2)}) collective-permute-start(bf16[8,288,128]{2,1,0:T(8,128)(2,1)S(1)} %all-to-all-done.own), channel_id=1, source_target_pairs={{0,8},{1,9},{2,10},{3,11},{4,12},{5,13},{6,14},{7,15},{8,0},{9,1},... | collective-permute-start | bytes 1769480 | tf_op jit(solution)/shard_map/ppermute | solution.py:283
  32.4 1.9 %collective-permute-start.8 = (bf16[576,128]{1,0:T(8,128)(2,1)}, bf16[576,128]{1,0:T(8,128)(2,1)S(1)}, u32[]{:S(2)}, u32[]{:S(2)}) collective-permute-start(bf16[576,128]{1,0:T(8,128)(2,1)} %get-tuple-element.8.win), channel_id=1, source_target_pairs={{0,8},{1,9},{2,10},{3,11},{4,12},{5,13},{6,14},{7,15},{8,0},{9,1},... | collective-permute-start | bytes 442376 | tf_op jit(solution)/shard_map/ppermute | solution.py:283
  34.3 0.0 collective-permute-done.7.w4
  34.3 5.6 %collective-permute-start.9 = (bf16[576,128]{1,0:T(8,128)(2,1)S(1)}, bf16[576,128]{1,0:T(8,128)(2,1)S(1)}, u32[]{:S(2)}, u32[]{:S(2)}) collective-permute-start(bf16[576,128]{1,0:T(8,128)(2,1)S(1)} %collective-permute-done.7.w4), channel_id=1, source_target_pairs={{0,8},{1,9},{2,10},{3,11},{4,12},{5,13},{6,14},{7,15},{8,0},{9,1},... | collective-permute-start | bytes 442376 | tf_op jit(solution)/shard_map/ppermute | solution.py:283
  39.9 7.6 %collective-permute-done.8.zv = bf16[576,128]{1,0:T(8,128)(2,1)S(1)} collective-permute-done((bf16[576,128]{1,0:T(8,128)(2,1)}, bf16[576,128]{1,0:T(8,128)(2,1)S(1)}, u32[]{:S(2)}, u32[]{:S(2)}) %collective-permute-start.8) | collective-permute-done | bytes 147488 | tf_op jit(solution)/shard_map/ppermute | solution.py:283
  47.5 3.1 %collective-permute-done.9.zw = bf16[576,128]{1,0:T(8,128)(2,1)S(1)} collective-permute-done((bf16[576,128]{1,0:T(8,128)(2,1)S(1)}, bf16[576,128]{1,0:T(8,128)(2,1)S(1)}, u32[]{:S(2)}, u32[]{:S(2)}) %collective-permute-start.9) | collective-permute-done | bytes 147488 | tf_op jit(solution)/shard_map/ppermute | solution.py:283
  50.6 0.9 pad_maximum_fusion
  51.5 4.3 %collective-permute-start.10 = (bf16[2304,128]{1,0:T(8,128)(2,1)S(1)}, bf16[2304,128]{1,0:T(8,128)(2,1)S(1)}, u32[]{:S(2)}, u32[]{:S(2)}) collective-permute-start(bf16[2304,128]{1,0:T(8,128)(2,1)S(1)} %pad_maximum_fusion), channel_id=1, source_target_pairs={{0,256},{256,0},{1,257},{257,1},{2,258},{258,2},{3,259},{259,3},{4... | collective-permute-start | bytes 1769480 | tf_op jit(solution)/shard_map/ppermute | solution.py:283
  55.9 1.9 %collective-permute-start.5 = (bf16[8,288,128]{2,1,0:T(8,128)(2,1)S(1)}, bf16[8,288,128]{2,1,0:T(8,128)(2,1)S(1)}, u32[]{:S(2)}, u32[]{:S(2)}) collective-permute-start(bf16[8,288,128]{2,1,0:T(8,128)(2,1)S(1)} %all-to-all-done.own), channel_id=1, source_target_pairs={{0,256},{256,0},{1,257},{257,1},{2,258},{258,2},{3,259},{259,3},{4... | collective-permute-start | bytes 1769480 | tf_op jit(solution)/shard_map/ppermute | solution.py:283
  57.8 0.0 collective-permute-done.4.far
  57.8 2.4 %collective-permute-start.6 = (bf16[8,288,128]{2,1,0:T(8,128)(2,1)S(1)}, bf16[8,288,128]{2,1,0:T(8,128)(2,1)S(1)}, u32[]{:S(2)}, u32[]{:S(2)}) collective-permute-start(bf16[8,288,128]{2,1,0:T(8,128)(2,1)S(1)} %collective-permute-done.4.far), channel_id=1, source_target_pairs={{0,256},{256,0},{1,257},{257,1},{2,258},{258,2},{3,259},{259,3},{4... | collective-permute-start | bytes 1769480 | tf_op jit(solution)/shard_map/ppermute | solution.py:283
  60.2 0.0 copy-done
  60.2 1.9 %collective-permute-start.1 = (bf16[1440,128]{1,0:T(8,128)(2,1)S(1)}, bf16[1440,128]{1,0:T(8,128)(2,1)S(1)}, u32[]{:S(2)}, u32[]{:S(2)}) collective-permute-start(bf16[1440,128]{1,0:T(8,128)(2,1)S(1)} %copy-done), channel_id=1, source_target_pairs={{0,2},{1,3},{2,0},{3,1},{4,6},{5,7},{6,4},{7,5},{8,10},{9,11},{10,... | collective-permute-start | bytes 1105928 | tf_op jit(solution)/shard_map/ppermute | solution.py:283
  62.1 1.9 %collective-permute-start = (bf16[1440,128]{1,0:T(8,128)(2,1)S(1)}, bf16[1440,128]{1,0:T(8,128)(2,1)S(1)}, u32[]{:S(2)}, u32[]{:S(2)}) collective-permute-start(bf16[1440,128]{1,0:T(8,128)(2,1)S(1)} %copy-done), channel_id=1, source_target_pairs={{0,1},{1,0},{2,3},{3,2},{4,5},{5,4},{6,7},{7,6},{8,9},{9,8},{10,11... | collective-permute-start | bytes 1105928 | tf_op jit(solution)/shard_map/ppermute | solution.py:283
  64.1 16.4 %collective-permute-done.1.e2 = bf16[1440,128]{1,0:T(8,128)(2,1)S(1)} collective-permute-done((bf16[1440,128]{1,0:T(8,128)(2,1)S(1)}, bf16[1440,128]{1,0:T(8,128)(2,1)S(1)}, u32[]{:S(2)}, u32[]{:S(2)}) %collective-permute-start.1) | collective-permute-done | bytes 368672 | tf_op jit(solution)/shard_map/ppermute | solution.py:283
  80.5 0.7 collective-permute-start.2
  81.1 0.0 collective-permute-done.10.pxw
  81.2 1.3 %collective-permute-start.3 = (bf16[1440,128]{1,0:T(8,128)(2,1)S(1)}, bf16[1440,128]{1,0:T(8,128)(2,1)S(1)}, u32[]{:S(2)}, u32[]{:S(2)}) collective-permute-start(bf16[1440,128]{1,0:T(8,128)(2,1)S(1)} %collective-permute-done.1.e2), channel_id=1, source_target_pairs={{1,0},{2,3},{5,4},{6,7},{9,8},{10,11},{13,12},{14,15},{17,16},{18,... | collective-permute-start | bytes 1105928 | tf_op jit(solution)/shard_map/ppermute | solution.py:283
  82.5 0.0 collective-permute-done.5.p_own
  82.5 0.0 collective-permute-done.6.p_far
  82.5 0.0 copy-done.1
  82.5 8.1 %series.1.factor = bf16[768,768]{1,0:T(8,128)(2,1)S(1)} custom-call(bf16[8,288,128]{2,1,0:T(8,128)(2,1)S(1)} %all-to-all-done.own, bf16[8,288,128]{2,1,0:T(8,128)(2,1)S(1)} %collective-permute-done.4.far, bf16[8,288,128]{2,1,0:T(8,128)(2,1)S(1)} %collective-permute-done.5.p_own, bf16[8,288,128]{2,1,0:T(8,128)(2,1)S(1)} %collective-permute-done.6.p_far, ...), custom_call_target="tpu_custom_call" | custom-call | flops 6000000000 | bytes 6000000 | tf_op jit(solution)/shard_map/series/pallas_call | solution.py:217
  90.5 0.0 collective-permute-done.e1
  90.6 0.0 collective-permute-done.2.near
  90.6 2.1 %collective-permute-done.3.relayed = bf16[1440,128]{1,0:T(8,128)(2,1)S(1)} collective-permute-done((bf16[1440,128]{1,0:T(8,128)(2,1)S(1)}, bf16[1440,128]{1,0:T(8,128)(2,1)S(1)}, u32[]{:S(2)}, u32[]{:S(2)}) %collective-permute-start.3) | collective-permute-done | bytes 368672 | tf_op jit(solution)/shard_map/ppermute | solution.py:283
  92.7 2.7 %update.1 = bf16[960,768]{1,0:T(8,128)(2,1)} custom-call(bf16[1440,128]{1,0:T(8,128)(2,1)S(1)} %copy-done, bf16[1440,128]{1,0:T(8,128)(2,1)S(1)} %collective-permute-done.e1, bf16[1440,128]{1,0:T(8,128)(2,1)S(1)} %collective-permute-done.1.e2, bf16[1440,128]{1,0:T(8,128)(2,1)S(1)} %collective-permute-done.2.near, ...), custom_call_target="tpu_custom_call" | custom-call | flops 1130000000 | bytes 4000000 | tf_op jit(solution)/shard_map/update/pallas_call | solution.py:270
Async XLA Ops:
  2.6 24.3 %all-to-all-start = ((bf16[8,288,128]{2,1,0:T(8,128)(2,1)}), bf16[8,288,128]{2,1,0:T(8,128)(2,1)S(1)}, u32[]{:S(2)}, u32[]{:S(2)}) async-start(bf16[8,288,128]{2,1,0:T(8,128)(2,1)} %shard_map.29), calls=%async_computation | async-start | bytes 1179648 | tf_op jit(solution)/shard_map/all_to_all | solution.py:292
  13.2 47.0 %copy-start = (bf16[1440,128]{1,0:T(8,128)(2,1)S(1)}, bf16[1440,128]{1,0:T(8,128)(2,1)}, u32[]{:S(2)}) copy-start(bf16[1440,128]{1,0:T(8,128)(2,1)} %get-tuple-element.7.e0) | copy-start | bytes 1105924
  13.2 69.3 %copy-start.1 = (bf16[576,128]{1,0:T(8,128)(2,1)S(1)}, bf16[576,128]{1,0:T(8,128)(2,1)}, u32[]{:S(2)}) copy-start(bf16[576,128]{1,0:T(8,128)(2,1)} %get-tuple-element.8.win) | copy-start | bytes 442372
  13.2 21.1 %collective-permute-start.7 = (bf16[576,128]{1,0:T(8,128)(2,1)}, bf16[576,128]{1,0:T(8,128)(2,1)S(1)}, u32[]{:S(2)}, u32[]{:S(2)}) collective-permute-start(bf16[576,128]{1,0:T(8,128)(2,1)} %get-tuple-element.8.win), channel_id=1, source_target_pairs={{0,4},{1,5},{2,6},{3,7},{4,0},{5,1},{6,2},{7,3},{8,12},{9,13},{10,... | collective-permute-start | bytes 442376 | tf_op jit(solution)/shard_map/ppermute | solution.py:283
  26.9 30.9 %collective-permute-start.4 = (bf16[8,288,128]{2,1,0:T(8,128)(2,1)S(1)}, bf16[8,288,128]{2,1,0:T(8,128)(2,1)S(1)}, u32[]{:S(2)}, u32[]{:S(2)}) collective-permute-start(bf16[8,288,128]{2,1,0:T(8,128)(2,1)S(1)} %all-to-all-done.own), channel_id=1, source_target_pairs={{0,8},{1,9},{2,10},{3,11},{4,12},{5,13},{6,14},{7,15},{8,0},{9,1},... | collective-permute-start | bytes 1769480 | tf_op jit(solution)/shard_map/ppermute | solution.py:283
  32.4 15.1 %collective-permute-start.8 = (bf16[576,128]{1,0:T(8,128)(2,1)}, bf16[576,128]{1,0:T(8,128)(2,1)S(1)}, u32[]{:S(2)}, u32[]{:S(2)}) collective-permute-start(bf16[576,128]{1,0:T(8,128)(2,1)} %get-tuple-element.8.win), channel_id=1, source_target_pairs={{0,8},{1,9},{2,10},{3,11},{4,12},{5,13},{6,14},{7,15},{8,0},{9,1},... | collective-permute-start | bytes 442376 | tf_op jit(solution)/shard_map/ppermute | solution.py:283
  34.3 16.2 %collective-permute-start.9 = (bf16[576,128]{1,0:T(8,128)(2,1)S(1)}, bf16[576,128]{1,0:T(8,128)(2,1)S(1)}, u32[]{:S(2)}, u32[]{:S(2)}) collective-permute-start(bf16[576,128]{1,0:T(8,128)(2,1)S(1)} %collective-permute-done.7.w4), channel_id=1, source_target_pairs={{0,8},{1,9},{2,10},{3,11},{4,12},{5,13},{6,14},{7,15},{8,0},{9,1},... | collective-permute-start | bytes 442376 | tf_op jit(solution)/shard_map/ppermute | solution.py:283
  51.5 29.6 %collective-permute-start.10 = (bf16[2304,128]{1,0:T(8,128)(2,1)S(1)}, bf16[2304,128]{1,0:T(8,128)(2,1)S(1)}, u32[]{:S(2)}, u32[]{:S(2)}) collective-permute-start(bf16[2304,128]{1,0:T(8,128)(2,1)S(1)} %pad_maximum_fusion), channel_id=1, source_target_pairs={{0,256},{256,0},{1,257},{257,1},{2,258},{258,2},{3,259},{259,3},{4... | collective-permute-start | bytes 1769480 | tf_op jit(solution)/shard_map/ppermute | solution.py:283
  55.9 26.6 %collective-permute-start.5 = (bf16[8,288,128]{2,1,0:T(8,128)(2,1)S(1)}, bf16[8,288,128]{2,1,0:T(8,128)(2,1)S(1)}, u32[]{:S(2)}, u32[]{:S(2)}) collective-permute-start(bf16[8,288,128]{2,1,0:T(8,128)(2,1)S(1)} %all-to-all-done.own), channel_id=1, source_target_pairs={{0,256},{256,0},{1,257},{257,1},{2,258},{258,2},{3,259},{259,3},{4... | collective-permute-start | bytes 1769480 | tf_op jit(solution)/shard_map/ppermute | solution.py:283
  57.8 24.7 %collective-permute-start.6 = (bf16[8,288,128]{2,1,0:T(8,128)(2,1)S(1)}, bf16[8,288,128]{2,1,0:T(8,128)(2,1)S(1)}, u32[]{:S(2)}, u32[]{:S(2)}) collective-permute-start(bf16[8,288,128]{2,1,0:T(8,128)(2,1)S(1)} %collective-permute-done.4.far), channel_id=1, source_target_pairs={{0,256},{256,0},{1,257},{257,1},{2,258},{258,2},{3,259},{259,3},{4... | collective-permute-start | bytes 1769480 | tf_op jit(solution)/shard_map/ppermute | solution.py:283
  60.2 20.2 %collective-permute-start.1 = (bf16[1440,128]{1,0:T(8,128)(2,1)S(1)}, bf16[1440,128]{1,0:T(8,128)(2,1)S(1)}, u32[]{:S(2)}, u32[]{:S(2)}) collective-permute-start(bf16[1440,128]{1,0:T(8,128)(2,1)S(1)} %copy-done), channel_id=1, source_target_pairs={{0,2},{1,3},{2,0},{3,1},{4,6},{5,7},{6,4},{7,5},{8,10},{9,11},{10,... | collective-permute-start | bytes 1105928 | tf_op jit(solution)/shard_map/ppermute | solution.py:283
  62.1 28.4 %collective-permute-start = (bf16[1440,128]{1,0:T(8,128)(2,1)S(1)}, bf16[1440,128]{1,0:T(8,128)(2,1)S(1)}, u32[]{:S(2)}, u32[]{:S(2)}) collective-permute-start(bf16[1440,128]{1,0:T(8,128)(2,1)S(1)} %copy-done), channel_id=1, source_target_pairs={{0,1},{1,0},{2,3},{3,2},{4,5},{5,4},{6,7},{7,6},{8,9},{9,8},{10,11... | collective-permute-start | bytes 1105928 | tf_op jit(solution)/shard_map/ppermute | solution.py:283
  80.5 10.1 %collective-permute-start.2 = (bf16[1440,128]{1,0:T(8,128)(2,1)S(1)}, bf16[1440,128]{1,0:T(8,128)(2,1)S(1)}, u32[]{:S(2)}, u32[]{:S(2)}) collective-permute-start(bf16[1440,128]{1,0:T(8,128)(2,1)S(1)} %copy-done), channel_id=1, source_target_pairs={{1,2},{2,1},{5,6},{6,5},{9,10},{10,9},{13,14},{14,13},{17,18},{18,... | collective-permute-start | bytes 1105928 | tf_op jit(solution)/shard_map/ppermute | solution.py:283
  81.2 11.5 %collective-permute-start.3 = (bf16[1440,128]{1,0:T(8,128)(2,1)S(1)}, bf16[1440,128]{1,0:T(8,128)(2,1)S(1)}, u32[]{:S(2)}, u32[]{:S(2)}) collective-permute-start(bf16[1440,128]{1,0:T(8,128)(2,1)S(1)} %collective-permute-done.1.e2), channel_id=1, source_target_pairs={{1,0},{2,3},{5,4},{6,7},{9,8},{10,11},{13,12},{14,15},{17,16},{18,... | collective-permute-start | bytes 1105928 | tf_op jit(solution)/shard_map/ppermute | solution.py:283
where the time goes:
time: 96 us; the launch traced here: 95.4 us
  starting transfers between devices  42.4 us (44%)
  waiting for transfers between devices  35.5 us (37%)
  Pallas kernels  16.3 us (17%)
    ppermute x11, starting transfers between devices, permute(): return lax.ppermute(value, axis, pairs)  34.8 us
    ppermute x11, waiting for transfers between devices, permute(): return lax.ppermute(value, axis, pairs)  29.2 us
    pallas_call x1, Pallas kernels, series(): pl.pallas_call(series_kernel, in_specs=[vmem] * len(lists), out_specs=vme...  8.05 us
    all_to_all x1, starting transfers between devices, ring_gather(): lax.all_to_all(copies, 'tile', 0, 0, axis_index_groups=groups, tiled=True)  7.64 us
    all_to_all x1, waiting for transfers between devices, ring_gather(): lax.all_to_all(copies, 'tile', 0, 0, axis_index_groups=groups, tiled=True)  6.33 us
    pallas_call x1, Pallas kernels, extract_edges(): return extraction(edges_kernel, specs, shapes, cost)(face, *[tile] * 6)  2.94 us
    pallas_call x1, Pallas kernels, update(): pl.pallas_call(update_kernel, in_specs=[vmem] * (len(chunks) + 1), out_sp...  2.71 us
    pallas_call x1, Pallas kernels, extract_shared(): extraction(shared_kernel, specs, [(RING, TILE_ROWS, LANES)], cost)  2.6 us
  transfers between devices with their start and end apart: 12, of which 5 were waited for; matrix products, arithmetic and copies ran while one was open for 1% of the time, Pallas kernels for 12%

commit v1 on v0

--- a/solution.py
+++ b/solution.py
@@ -141,9 +141,10 @@
 
 def place_tile(source, n, target, rests, row, col, own_col):
     lanes = pl.ds(main_at(col, own_col), LANES)
-    target[pl.ds(main_at(row, own_col), LANES), lanes] = source[n, :LANES]
-    target[pl.ds(rest_at(row, own_col), 64), lanes] = source[n, LANES:PIECE]
-    rests[row, col] = source[n, PIECE:]
+    base = n * TILE_ROWS
+    target[pl.ds(main_at(row, own_col), LANES), lanes] = source[base : base + LANES, :]
+    target[pl.ds(rest_at(row, own_col), 64), lanes] = source[base + LANES : base + PIECE, :]
+    rests[row, col] = source[base + PIECE : base + TILE_ROWS, :]
 
 
 def join_rests(target, rests, own_col):
@@ -164,7 +165,7 @@
     lax.fori_loop(0, 8, body, 0)
 
 
-def series_kernel(own, far, p_own, p_far, win, w4, zv, zw, pxw, out, *scratch):
+def series_kernel(own, far, p_own, p_far, win, w4, zv, zw, out, *scratch):
     mine, other, rests, power, power2, start_a, total = scratch
     pair, tile = here()
     z = tile >> 3
@@ -186,9 +187,10 @@
                 target[pl.ds(main_at(row, own_col), LANES), lanes] = source[at : at + LANES, :]
                 target[pl.ds(rest_at(row, own_col), 64), lanes] = source[at + LANES : at + PIECE, :]
 
+    base = RING * TILE_ROWS
     win_sources = (
         [(x, 0) for x in (win, w4, zv, zw)],
-        [(pxw, n * WIN_ROWS) for n in range(4)],
+        [(x, base + n * WIN_ROWS) for n, x in ((0, p_own), (0, p_far), (1, p_own), (1, p_far))],
     )
     place(mine, own, far)
     place(other, p_own, p_far)
@@ -234,7 +236,7 @@
     )(*lists)
 
 
-def update_kernel(e0, e1, e2, near, relayed, factor, out, matrix):
+def update_kernel(e0, e1, to_inner, to_outer, near, relayed, factor, out, matrix, held, done):
     col = here()[1] & 3
     inner = ((col ^ (col >> 1)) & 1) == 1
     left = (lax.broadcasted_iota(jnp.int32, (HALF, LANES), 1) < 64) ^ ((col & 1) == 1)
@@ -254,15 +256,20 @@
 
     @pl.when(inner)
     def _():
-        fill(1, e2, near)
+        fill(1, to_inner, near)
 
     @pl.when(jnp.logical_not(inner))
     def _():
-        fill(1, e2, relayed)
-
+        fill(1, to_outer, relayed)
+
+    copies = []
     for m in range(2):
         rows = slice(m * main // 2, (m + 1) * main // 2)
-        out[rows, :] = (dot(matrix[rows, :], factor[...]) * math.sqrt(FACE)).astype(jnp.bfloat16)
+        held[rows, :] = (dot(matrix[rows, :], factor[...]) * math.sqrt(FACE)).astype(jnp.bfloat16)
+        copies.append(pltpu.make_async_copy(held.at[rows, :], out.at[rows, :], done.at[m]))
+        copies[-1].start()
+    for copy in copies:
+        copy.wait()
 
 
 def update(chunks, factor):
@@ -270,9 +277,9 @@
     return pl.pallas_call(
         update_kernel,
         in_specs=[vmem] * (len(chunks) + 1),
-        out_specs=vmem,
+        out_specs=pl.BlockSpec(memory_space=pl.ANY),
         out_shape=jax.ShapeDtypeStruct((EXT * PIECE, FACE), jnp.bfloat16),
-        scratch_shapes=[pltpu.VMEM((EXT * PIECE, FACE), jnp.bfloat16)],
+        scratch_shapes=[pltpu.VMEM((EXT * PIECE, FACE), jnp.bfloat16)] * 2 + [pltpu.SemaphoreType.DMA((2,))],
         cost_estimate=pl.CostEstimate(flops=1130 * 10**6, bytes_accessed=4 * 10**6, transcendentals=0),
         compiler_params=pltpu.CompilerParams(vmem_limit_bytes=32 * 2**20),
         name="update",
@@ -302,18 +309,19 @@
     own = ring_gather(extract_shared(child_maps[0, 0], face_order[0]))
     win, ext = extract_edges(child_maps[0, 0], face_order[0])
     w4 = permute(win, masked(4))
-    e2 = permute(ext, masked(2))
+    to_inner = permute(ext, in_rows(((0, 2), (3, 1))))
+    to_outer = permute(ext, in_rows(((2, 0), (1, 3))))
     zv = permute(win, masked(8))
     zw = permute(w4, masked(8))
     e1 = permute(ext, masked(1))
-    pxw = permute(jnp.concatenate([win, w4, zv, zw]), partner, "pair")
     far = permute(own, masked(8))
-    p_own = permute(own, partner, "pair")
-    p_far = permute(far, partner, "pair")
+    flat = (RING * TILE_ROWS, LANES)
+    pa = permute(jnp.concatenate([own.reshape(flat), win, zv]), partner, "pair")
+    pb = permute(jnp.concatenate([far.reshape(flat), w4, zw]), partner, "pair")
     near = permute(ext, inner)
-    relayed = permute(e2, outer)
-    factor = series([own, far, p_own, p_far, win, w4, zv, zw, pxw])
-    return update([ext, e1, e2, near, relayed], factor)[None, None]
+    relayed = permute(to_inner, outer)
+    factor = series([own.reshape(flat), far.reshape(flat), pa, pb, win, w4, zv, zw])
+    return update([ext, e1, to_inner, to_outer, near, relayed], factor)[None, None]
 
 
 def solution(mesh):

time: 96 us -> 84 us (0.88)
  waiting for transfers between devices: 35.5 us -> 20.7 us
  starting transfers between devices: 42.4 us -> 45.4 us
    ppermute x11, waiting for transfers between devices: 29.2 us -> 18.2 us  [permute(): return lax.ppermute(value, axis, pairs)]
    all_to_all x1, waiting for transfers between devices: 6.33 us -> 2.47 us  [ring_gather(): lax.all_to_all(copies, 'tile', 0, 0, axis_index_groups=groups, tiled=True)]
    ppermute x11, starting transfers between devices: 34.8 us -> 37.7 us  [permute(): return lax.ppermute(value, axis, pairs)]
  transfers between devices with their start and end apart: 12 -> 12, of which waited for: 5 -> 5; matrix products, arithmetic and copies ran while one was open for 1% -> 1% of each run, Pallas kernels for 12% -> 13%
where the time goes in v1:
time: 84 us; the launch traced here: 83.4 us
  starting transfers between devices  45.4 us (54%)
  waiting for transfers between devices  20.7 us (25%)
  Pallas kernels  16.1 us (19%)
  other arithmetic  1.09 us (1%)
    ppermute x11, starting transfers between devices, permute(): return lax.ppermute(value, axis, pairs)  37.7 us
    ppermute x11, waiting for transfers between devices, permute(): return lax.ppermute(value, axis, pairs)  18.2 us
    pallas_call x1, Pallas kernels, series(): pl.pallas_call(series_kernel, in_specs=[vmem] * len(lists), out_specs=vme...  8.05 us
    all_to_all x1, starting transfers between devices, ring_gather(): lax.all_to_all(copies, 'tile', 0, 0, axis_index_groups=groups, tiled=True)  7.64 us
    pallas_call x1, Pallas kernels, extract_edges(): return extraction(edges_kernel, specs, shapes, cost)(face, *[tile] * 6)  2.94 us
    pallas_call x1, Pallas kernels, extract_shared(): extraction(shared_kernel, specs, [(RING, TILE_ROWS, LANES)], cost)  2.6 us
    all_to_all x1, waiting for transfers between devices, ring_gather(): lax.all_to_all(copies, 'tile', 0, 0, axis_index_groups=groups, tiled=True)  2.47 us
    pallas_call x1, Pallas kernels, update(): pl.pallas_call(update_kernel, in_specs=[vmem] * (len(chunks) + 1), out_sp...  2.46 us
  transfers between devices with their start and end apart: 12, of which 5 were waited for; matrix products, arithmetic and copies ran while one was open for 1% of the time, Pallas kernels for 13%

profile of v1, /device:TPU:1, one launch (start us, length us, event | category | flops | bytes accessed | tf_op | source)
XLA Modules:
  0.0 83.4 jit_solution(16601825766780768768)
XLA Ops:
  0.0 2.6 %shard_map.29 = bf16[8,288,128]{2,1,0:T(8,128)(2,1)} custom-call(s32[2,6]{1,0:T(2,128)} %bitcast.17, bf16[1152,1152]{1,0:T(8,128)(2,1)} %bitcast.9, bf16[1152,1152]{1,0:T(8,128)(2,1)} %bitcast.10), custom_call_target="tpu_custom_call" | custom-call | flops 30000000 | bytes 1000000 | tf_op jit(solution)/shard_map/pallas_call | solution.py:119
  2.6 7.6 %all-to-all-start = ((bf16[8,288,128]{2,1,0:T(8,128)(2,1)}), bf16[8,288,128]{2,1,0:T(8,128)(2,1)S(1)}, u32[]{:S(2)}, u32[]{:S(2)}) async-start(bf16[8,288,128]{2,1,0:T(8,128)(2,1)} %shard_map.29), calls=%async_computation | async-start | bytes 1179648 | tf_op jit(solution)/shard_map/all_to_all | solution.py:299
  10.2 2.9 %shard_map.28 = (bf16[576,128]{1,0:T(8,128)(2,1)}, bf16[1440,128]{1,0:T(8,128)(2,1)}) custom-call(s32[2,6]{1,0:T(2,128)} %bitcast.18, bf16[1152,1152]{1,0:T(8,128)(2,1)} %bitcast.11, bf16[1152,1152]{1,0:T(8,128)(2,1)} %bitcast.12, bf16[1152,1152]{1,0:T(8,128)(2,1)} %bitcast.13, bf16[1152,1152]{1,0:T(8,128)(2,1)} %bitcast.14, bf16[1152,1152]{1,0:T(8,128)(2,1)} %bitcast.15, ...), custom_call_target="tpu_custom_call" | custom-call | flops 400000000 | bytes 2000000 | tf_op jit(solution)/shard_map/pallas_call | solution.py:127
  13.2 7.3 %collective-permute-start.8 = (bf16[576,128]{1,0:T(8,128)(2,1)}, bf16[576,128]{1,0:T(8,128)(2,1)S(1)}, u32[]{:S(2)}, u32[]{:S(2)}) collective-permute-start(bf16[576,128]{1,0:T(8,128)(2,1)} %get-tuple-element.8.win), channel_id=1, source_target_pairs={{0,4},{1,5},{2,6},{3,7},{4,0},{5,1},{6,2},{7,3},{8,12},{9,13},{10,... | collective-permute-start | bytes 442376 | tf_op jit(solution)/shard_map/ppermute | solution.py:290
  20.5 4.0 %collective-permute-start.6 = (bf16[576,128]{1,0:T(8,128)(2,1)}, bf16[576,128]{1,0:T(8,128)(2,1)S(1)}, u32[]{:S(2)}, u32[]{:S(2)}) collective-permute-start(bf16[576,128]{1,0:T(8,128)(2,1)} %get-tuple-element.8.win), channel_id=1, source_target_pairs={{0,8},{1,9},{2,10},{3,11},{4,12},{5,13},{6,14},{7,15},{8,0},{9,1},... | collective-permute-start | bytes 442376 | tf_op jit(solution)/shard_map/ppermute | solution.py:290
  24.5 2.5 %all-to-all-done = bf16[8,288,128]{2,1,0:T(8,128)(2,1)S(1)} async-done(((bf16[8,288,128]{2,1,0:T(8,128)(2,1)}), bf16[8,288,128]{2,1,0:T(8,128)(2,1)S(1)}, u32[]{:S(2)}, u32[]{:S(2)}) %all-to-all-start) | async-done | bytes 589856 | tf_op jit(solution)/shard_map/all_to_all | solution.py:299
  26.9 5.5 %collective-permute-start.5 = (bf16[8,288,128]{2,1,0:T(8,128)(2,1)S(1)}, bf16[8,288,128]{2,1,0:T(8,128)(2,1)S(1)}, u32[]{:S(2)}, u32[]{:S(2)}) collective-permute-start(bf16[8,288,128]{2,1,0:T(8,128)(2,1)S(1)} %all-to-all-done), channel_id=1, source_target_pairs={{0,8},{1,9},{2,10},{3,11},{4,12},{5,13},{6,14},{7,15},{8,0},{9,1},... | collective-permute-start | bytes 1769480 | tf_op jit(solution)/shard_map/ppermute | solution.py:290
  32.4 0.0 collective-permute-done.8.w4
  32.4 7.5 %collective-permute-start.9 = (bf16[576,128]{1,0:T(8,128)(2,1)S(1)}, bf16[576,128]{1,0:T(8,128)(2,1)S(1)}, u32[]{:S(2)}, u32[]{:S(2)}) collective-permute-start(bf16[576,128]{1,0:T(8,128)(2,1)S(1)} %collective-permute-done.8.w4), channel_id=1, source_target_pairs={{0,8},{1,9},{2,10},{3,11},{4,12},{5,13},{6,14},{7,15},{8,0},{9,1},... | collective-permute-start | bytes 442376 | tf_op jit(solution)/shard_map/ppermute | solution.py:290
  39.9 0.0 collective-permute-done.6.zv
  39.9 0.0 copy-start
  39.9 0.0 copy-start.1
  40.0 1.0 %pad_maximum_fusion = bf16[3456,128]{1,0:T(8,128)(2,1)S(1)} fusion(bf16[576,128]{1,0:T(8,128)(2,1)S(1)} %collective-permute-done.6.zv, bf16[576,128]{1,0:T(8,128)(2,1)} %get-tuple-element.8.win, bf16[2304,128]{1,0:T(8,128)(2,1)S(1)} %bitcast.5), kind=kLoop, calls=%fused_computation | loop fusion | flops 2654208 | bytes 1769472 | tf_op jit(solution)/shard_map/concatenate | solution.py:319
  41.0 2.7 %collective-permute-start.7 = (bf16[3456,128]{1,0:T(8,128)(2,1)S(1)}, bf16[3456,128]{1,0:T(8,128)(2,1)S(1)}, u32[]{:S(2)}, u32[]{:S(2)}) collective-permute-start(bf16[3456,128]{1,0:T(8,128)(2,1)S(1)} %pad_maximum_fusion), channel_id=1, source_target_pairs={{0,256},{256,0},{1,257},{257,1},{2,258},{258,2},{3,259},{259,3},{4... | collective-permute-start | bytes 2654216 | tf_op jit(solution)/shard_map/ppermute | solution.py:290
  43.7 3.8 %collective-permute-done.9.zw = bf16[576,128]{1,0:T(8,128)(2,1)S(1)} collective-permute-done((bf16[576,128]{1,0:T(8,128)(2,1)S(1)}, bf16[576,128]{1,0:T(8,128)(2,1)S(1)}, u32[]{:S(2)}, u32[]{:S(2)}) %collective-permute-start.9) | collective-permute-done | bytes 147488 | tf_op jit(solution)/shard_map/ppermute | solution.py:290
  47.5 0.0 collective-permute-done.5
  47.5 0.1 pad_maximum_fusion.1
  47.6 4.3 %collective-permute-start.10 = (bf16[3456,128]{1,0:T(8,128)(2,1)S(1)}, bf16[3456,128]{1,0:T(8,128)(2,1)S(1)}, u32[]{:S(2)}, u32[]{:S(2)}) collective-permute-start(bf16[3456,128]{1,0:T(8,128)(2,1)S(1)} %pad_maximum_fusion.1), channel_id=1, source_target_pairs={{0,256},{256,0},{1,257},{257,1},{2,258},{258,2},{3,259},{259,3},{4... | collective-permute-start | bytes 2654216 | tf_op jit(solution)/shard_map/ppermute | solution.py:290
  51.8 0.0 copy-done
  51.8 1.3 %collective-permute-start.1 = (bf16[1440,128]{1,0:T(8,128)(2,1)S(1)}, bf16[1440,128]{1,0:T(8,128)(2,1)S(1)}, u32[]{:S(2)}, u32[]{:S(2)}) collective-permute-start(bf16[1440,128]{1,0:T(8,128)(2,1)S(1)} %copy-done), channel_id=1, source_target_pairs={{0,2},{3,1},{4,6},{7,5},{8,10},{11,9},{12,14},{15,13},{16,18},{19,... | collective-permute-start | bytes 1105928 | tf_op jit(solution)/shard_map/ppermute | solution.py:290
  53.1 2.0 %collective-permute-start = (bf16[1440,128]{1,0:T(8,128)(2,1)S(1)}, bf16[1440,128]{1,0:T(8,128)(2,1)S(1)}, u32[]{:S(2)}, u32[]{:S(2)}) collective-permute-start(bf16[1440,128]{1,0:T(8,128)(2,1)S(1)} %copy-done), channel_id=1, source_target_pairs={{0,1},{1,0},{2,3},{3,2},{4,5},{5,4},{6,7},{7,6},{8,9},{9,8},{10,11... | collective-permute-start | bytes 1105928 | tf_op jit(solution)/shard_map/ppermute | solution.py:290
  55.2 1.3 %collective-permute-start.2 = (bf16[1440,128]{1,0:T(8,128)(2,1)S(1)}, bf16[1440,128]{1,0:T(8,128)(2,1)S(1)}, u32[]{:S(2)}, u32[]{:S(2)}) collective-permute-start(bf16[1440,128]{1,0:T(8,128)(2,1)S(1)} %copy-done), channel_id=1, source_target_pairs={{2,0},{1,3},{6,4},{5,7},{10,8},{9,11},{14,12},{13,15},{18,16},{17,... | collective-permute-start | bytes 1105928 | tf_op jit(solution)/shard_map/ppermute | solution.py:290
  56.5 4.9 %collective-permute-done.1.to_inner = bf16[1440,128]{1,0:T(8,128)(2,1)S(1)} collective-permute-done((bf16[1440,128]{1,0:T(8,128)(2,1)S(1)}, bf16[1440,128]{1,0:T(8,128)(2,1)S(1)}, u32[]{:S(2)}, u32[]{:S(2)}) %collective-permute-start.1) | collective-permute-done | bytes 368672 | tf_op jit(solution)/shard_map/ppermute | solution.py:290
  61.4 0.7 collective-permute-start.3
  62.0 0.0 collective-permute-done.7.p_own
  62.1 1.3 %collective-permute-start.4 = (bf16[1440,128]{1,0:T(8,128)(2,1)S(1)}, bf16[1440,128]{1,0:T(8,128)(2,1)S(1)}, u32[]{:S(2)}, u32[]{:S(2)}) collective-permute-start(bf16[1440,128]{1,0:T(8,128)(2,1)S(1)} %collective-permute-done.1.to_inner), channel_id=1, source_target_pairs={{1,0},{2,3},{5,4},{6,7},{9,8},{10,11},{13,12},{14,15},{17,16},{18,... | collective-permute-start | bytes 1105928 | tf_op jit(solution)/shard_map/ppermute | solution.py:290
  63.4 0.0 collective-permute-done.10.p_far
  63.4 0.0 copy-done.1
  63.4 8.1 %series.1.factor = bf16[768,768]{1,0:T(8,128)(2,1)S(1)} custom-call(bf16[2304,128]{1,0:T(8,128)(2,1)S(1)} %bitcast.6, bf16[2304,128]{1,0:T(8,128)(2,1)S(1)} %bitcast.8, bf16[3456,128]{1,0:T(8,128)(2,1)S(1)} %collective-permute-done.7.p_own, bf16[3456,128]{1,0:T(8,128)(2,1)S(1)} %collective-permute-done.10.p_far, bf16[576,128]{1,0:T(8,128)(2,1)S(1)} %copy-done.1, ...), custom_call_target="tpu_custom_call" | custom-call | flops 6000000000 | bytes 6000000 | tf_op jit(solution)/shard_map/series/pallas_call | solution.py:219
  71.4 0.0 collective-permute-done.e1
  71.4 1.5 %collective-permute-done.2.to_outer = bf16[1440,128]{1,0:T(8,128)(2,1)S(1)} collective-permute-done((bf16[1440,128]{1,0:T(8,128)(2,1)S(1)}, bf16[1440,128]{1,0:T(8,128)(2,1)S(1)}, u32[]{:S(2)}, u32[]{:S(2)}) %collective-permute-start.2) | collective-permute-done | bytes 368672 | tf_op jit(solution)/shard_map/ppermute | solution.py:290
  72.9 0.0 collective-permute-done.3.near
  72.9 8.0 %collective-permute-done.4.relayed = bf16[1440,128]{1,0:T(8,128)(2,1)S(1)} collective-permute-done((bf16[1440,128]{1,0:T(8,128)(2,1)S(1)}, bf16[1440,128]{1,0:T(8,128)(2,1)S(1)}, u32[]{:S(2)}, u32[]{:S(2)}) %collective-permute-start.4) | collective-permute-done | bytes 368672 | tf_op jit(solution)/shard_map/ppermute | solution.py:290
  81.0 2.5 %update.1 = bf16[960,768]{1,0:T(8,128)(2,1)} custom-call(bf16[1440,128]{1,0:T(8,128)(2,1)S(1)} %copy-done, bf16[1440,128]{1,0:T(8,128)(2,1)S(1)} %collective-permute-done.e1, bf16[1440,128]{1,0:T(8,128)(2,1)S(1)} %collective-permute-done.1.to_inner, bf16[1440,128]{1,0:T(8,128)(2,1)S(1)} %collective-permute-done.2.to_outer, ...), custom_call_target="tpu_custom_call" | custom-call | flops 1130000000 | bytes 4000000 | tf_op jit(solution)/shard_map/update/pallas_call | solution.py:277
Async XLA Ops:
  2.6 24.3 %all-to-all-start = ((bf16[8,288,128]{2,1,0:T(8,128)(2,1)}), bf16[8,288,128]{2,1,0:T(8,128)(2,1)S(1)}, u32[]{:S(2)}, u32[]{:S(2)}) async-start(bf16[8,288,128]{2,1,0:T(8,128)(2,1)} %shard_map.29), calls=%async_computation | async-start | bytes 1179648 | tf_op jit(solution)/shard_map/all_to_all | solution.py:299
  13.2 19.2 %collective-permute-start.8 = (bf16[576,128]{1,0:T(8,128)(2,1)}, bf16[576,128]{1,0:T(8,128)(2,1)S(1)}, u32[]{:S(2)}, u32[]{:S(2)}) collective-permute-start(bf16[576,128]{1,0:T(8,128)(2,1)} %get-tuple-element.8.win), channel_id=1, source_target_pairs={{0,4},{1,5},{2,6},{3,7},{4,0},{5,1},{6,2},{7,3},{8,12},{9,13},{10,... | collective-permute-start | bytes 442376 | tf_op jit(solution)/shard_map/ppermute | solution.py:290
  20.5 19.5 %collective-permute-start.6 = (bf16[576,128]{1,0:T(8,128)(2,1)}, bf16[576,128]{1,0:T(8,128)(2,1)S(1)}, u32[]{:S(2)}, u32[]{:S(2)}) collective-permute-start(bf16[576,128]{1,0:T(8,128)(2,1)} %get-tuple-element.8.win), channel_id=1, source_target_pairs={{0,8},{1,9},{2,10},{3,11},{4,12},{5,13},{6,14},{7,15},{8,0},{9,1},... | collective-permute-start | bytes 442376 | tf_op jit(solution)/shard_map/ppermute | solution.py:290
  26.9 20.5 %collective-permute-start.5 = (bf16[8,288,128]{2,1,0:T(8,128)(2,1)S(1)}, bf16[8,288,128]{2,1,0:T(8,128)(2,1)S(1)}, u32[]{:S(2)}, u32[]{:S(2)}) collective-permute-start(bf16[8,288,128]{2,1,0:T(8,128)(2,1)S(1)} %all-to-all-done), channel_id=1, source_target_pairs={{0,8},{1,9},{2,10},{3,11},{4,12},{5,13},{6,14},{7,15},{8,0},{9,1},... | collective-permute-start | bytes 1769480 | tf_op jit(solution)/shard_map/ppermute | solution.py:290
  32.4 15.1 %collective-permute-start.9 = (bf16[576,128]{1,0:T(8,128)(2,1)S(1)}, bf16[576,128]{1,0:T(8,128)(2,1)S(1)}, u32[]{:S(2)}, u32[]{:S(2)}) collective-permute-start(bf16[576,128]{1,0:T(8,128)(2,1)S(1)} %collective-permute-done.8.w4), channel_id=1, source_target_pairs={{0,8},{1,9},{2,10},{3,11},{4,12},{5,13},{6,14},{7,15},{8,0},{9,1},... | collective-permute-start | bytes 442376 | tf_op jit(solution)/shard_map/ppermute | solution.py:290
  39.9 11.9 %copy-start = (bf16[1440,128]{1,0:T(8,128)(2,1)S(1)}, bf16[1440,128]{1,0:T(8,128)(2,1)}, u32[]{:S(2)}) copy-start(bf16[1440,128]{1,0:T(8,128)(2,1)} %get-tuple-element.7.e0) | copy-start | bytes 1105924
  39.9 23.4 %copy-start.1 = (bf16[576,128]{1,0:T(8,128)(2,1)S(1)}, bf16[576,128]{1,0:T(8,128)(2,1)}, u32[]{:S(2)}) copy-start(bf16[576,128]{1,0:T(8,128)(2,1)} %get-tuple-element.8.win) | copy-start | bytes 442372
  41.0 21.1 %collective-permute-start.7 = (bf16[3456,128]{1,0:T(8,128)(2,1)S(1)}, bf16[3456,128]{1,0:T(8,128)(2,1)S(1)}, u32[]{:S(2)}, u32[]{:S(2)}) collective-permute-start(bf16[3456,128]{1,0:T(8,128)(2,1)S(1)} %pad_maximum_fusion), channel_id=1, source_target_pairs={{0,256},{256,0},{1,257},{257,1},{2,258},{258,2},{3,259},{259,3},{4... | collective-permute-start | bytes 2654216 | tf_op jit(solution)/shard_map/ppermute | solution.py:290
  47.6 15.8 %collective-permute-start.10 = (bf16[3456,128]{1,0:T(8,128)(2,1)S(1)}, bf16[3456,128]{1,0:T(8,128)(2,1)S(1)}, u32[]{:S(2)}, u32[]{:S(2)}) collective-permute-start(bf16[3456,128]{1,0:T(8,128)(2,1)S(1)} %pad_maximum_fusion.1), channel_id=1, source_target_pairs={{0,256},{256,0},{1,257},{257,1},{2,258},{258,2},{3,259},{259,3},{4... | collective-permute-start | bytes 2654216 | tf_op jit(solution)/shard_map/ppermute | solution.py:290
  51.8 9.5 %collective-permute-start.1 = (bf16[1440,128]{1,0:T(8,128)(2,1)S(1)}, bf16[1440,128]{1,0:T(8,128)(2,1)S(1)}, u32[]{:S(2)}, u32[]{:S(2)}) collective-permute-start(bf16[1440,128]{1,0:T(8,128)(2,1)S(1)} %copy-done), channel_id=1, source_target_pairs={{0,2},{3,1},{4,6},{7,5},{8,10},{11,9},{12,14},{15,13},{16,18},{19,... | collective-permute-start | bytes 1105928 | tf_op jit(solution)/shard_map/ppermute | solution.py:290
  53.1 18.3 %collective-permute-start = (bf16[1440,128]{1,0:T(8,128)(2,1)S(1)}, bf16[1440,128]{1,0:T(8,128)(2,1)S(1)}, u32[]{:S(2)}, u32[]{:S(2)}) collective-permute-start(bf16[1440,128]{1,0:T(8,128)(2,1)S(1)} %copy-done), channel_id=1, source_target_pairs={{0,1},{1,0},{2,3},{3,2},{4,5},{5,4},{6,7},{7,6},{8,9},{9,8},{10,11... | collective-permute-start | bytes 1105928 | tf_op jit(solution)/shard_map/ppermute | solution.py:290
  55.2 17.8 %collective-permute-start.2 = (bf16[1440,128]{1,0:T(8,128)(2,1)S(1)}, bf16[1440,128]{1,0:T(8,128)(2,1)S(1)}, u32[]{:S(2)}, u32[]{:S(2)}) collective-permute-start(bf16[1440,128]{1,0:T(8,128)(2,1)S(1)} %copy-done), channel_id=1, source_target_pairs={{2,0},{1,3},{6,4},{5,7},{10,8},{9,11},{14,12},{13,15},{18,16},{17,... | collective-permute-start | bytes 1105928 | tf_op jit(solution)/shard_map/ppermute | solution.py:290
  61.4 11.6 %collective-permute-start.3 = (bf16[1440,128]{1,0:T(8,128)(2,1)S(1)}, bf16[1440,128]{1,0:T(8,128)(2,1)S(1)}, u32[]{:S(2)}, u32[]{:S(2)}) collective-permute-start(bf16[1440,128]{1,0:T(8,128)(2,1)S(1)} %copy-done), channel_id=1, source_target_pairs={{1,2},{2,1},{5,6},{6,5},{9,10},{10,9},{13,14},{14,13},{17,18},{18,... | collective-permute-start | bytes 1105928 | tf_op jit(solution)/shard_map/ppermute | solution.py:290
  62.1 18.9 %collective-permute-start.4 = (bf16[1440,128]{1,0:T(8,128)(2,1)S(1)}, bf16[1440,128]{1,0:T(8,128)(2,1)S(1)}, u32[]{:S(2)}, u32[]{:S(2)}) collective-permute-start(bf16[1440,128]{1,0:T(8,128)(2,1)S(1)} %collective-permute-done.1.to_inner), channel_id=1, source_target_pairs={{1,0},{2,3},{5,4},{6,7},{9,8},{10,11},{13,12},{14,15},{17,16},{18,... | collective-permute-start | bytes 1105928 | tf_op jit(solution)/shard_map/ppermute | solution.py:290
